TPU v7x, 256 devices: a whole 4x4x8 slice. The times are simulated.
256 devices in a mesh: wide: 128 (over z, y, x), narrow: 2 (over core).
Axes of the slice: x: 4, y: 4, z: 8, core: 2. Of those that a mesh axis runs over, the one named last changes fastest.
Arguments:
- queries: bfloat16 [32768, 2048], P(('wide', 'narrow')), may hold values from -6 to 6
- keys: bfloat16 [32768, 2048], P(('wide', 'narrow')), may hold values from -6 to 6
- values: bfloat16 [32768, 2048], P(('wide', 'narrow')), may hold values from -6 to 6
Outputs:
- attended: bfloat16 [32768, 2048], P(('wide', 'narrow'))
All inputs are finite; a program needn't handle non-finite values.
Results may differ from a plain program's by a relative error of at most 0.008.
Values sent between devices are 32-bit elements; how exact they have to be, the bound alone decides.
A program may use at most 192 MiB of HBM per device.

v0:
```python
import jax
import jax.numpy as jnp
from jax import lax
from jax.sharding import PartitionSpec as P

HEADS = 16
HEAD_DIM = 128


def carried_in(value, axis, combine, identity):
    count, mine = (lax.axis_size(axis), lax.axis_index(axis))
    everything = lax.all_gather(value, axis)
    start = jnp.broadcast_to(jnp.asarray(identity, value.dtype), value.shape)

    def step(k, before):
        reached = k < mine
        new = combine(before, everything[k])
        return jnp.where(reached, new, before)

    return lax.fori_loop(0, count, step, start)


def add_states(earlier, later):
    return earlier + later


def shards(queries, keys, values):
    tokens = queries.shape[0]
    q_heads = queries.reshape(tokens, HEADS, HEAD_DIM)
    k_heads = keys.reshape(tokens, HEADS, HEAD_DIM)
    v_heads = values.reshape(tokens, HEADS, HEAD_DIM)
    own_state = jnp.einsum("shd,she->hde", k_heads, v_heads, preferred_element_type=jnp.float32)
    empty = jnp.zeros_like(own_state)
    below = carried_in(own_state, "narrow", add_states, empty)
    group_state = lax.psum_scatter(own_state, "narrow", scatter_dimension=0, tiled=True)
    outer_part = carried_in(group_state, "wide", add_states, jnp.zeros_like(group_state))
    outer_part = lax.all_gather(outer_part, "narrow", axis=0, tiled=True)
    carry = outer_part + below
    rows = jnp.arange(tokens, dtype=jnp.int32)
    causal = rows[None, :, None] >= rows[None, None, :]
    scores = jnp.einsum("thd,shd->hts", q_heads, k_heads, preferred_element_type=jnp.float32)
    scores = jnp.where(causal, scores, 0.0).astype(jnp.bfloat16)
    local = jnp.einsum("hts,shd->thd", scores, v_heads, preferred_element_type=jnp.float32)
    carry_high = carry.astype(jnp.bfloat16)
    carry_low = (carry - carry_high.astype(jnp.float32)).astype(jnp.bfloat16)
    carried = jnp.einsum("thd,hde->the", q_heads, carry_high, preferred_element_type=jnp.float32)
    carried = carried + jnp.einsum(
        "thd,hde->the", q_heads, carry_low, preferred_element_type=jnp.float32
    )
    total = local + carried
    factor = lax.rsqrt(jnp.mean(total * total, axis=-1, keepdims=True) + 1e-05)
    return (total * factor).astype(jnp.bfloat16).reshape(tokens, HEADS * HEAD_DIM)


def solution(mesh):
    placed = (P(("wide", "narrow"), None), P(("wide", "narrow"), None), P(("wide", "narrow"), None))
    return jax.shard_map(
        shards, mesh=mesh, in_specs=placed, out_specs=P(("wide", "narrow"), None), check_vma=False
    )
```

profile of v0, /device:TPU:225, one launch (start us, length us, event | category | flops | bytes accessed | tf_op | source)
XLA Modules:
  0.0 553.8 jit_solution(78602089080309038)
XLA Ops:
  6.5 1.4 copy.22
  7.9 2.3 fusion.4
  10.3 14.7 %reduce-scatter.2.cloned.1.call-done = f32[8,128,128]{2,1,0:T(8,128)} async-done(((f32[16,128,128]{2,1,0:T(8,128)}), f32[8,128,128]{2,1,0:T(8,128)}) %reduce-scatter.2.cloned.1.call-update) | async-done | bytes 524304 | tf_op jit(solution)/shard_map/reduce_scatter | solution.py:35
  25.9 341.0 %all-gather.8.cloned.1.call-done = f32[1024,128,128]{2,1,0:T(8,128)} async-done(((f32[8,128,128]{2,1,0:T(8,128)}), f32[1024,128,128]{2,1,0:T(8,128)}) %all-gather.8.cloned.1.call-update) | async-done | bytes 67108880 | tf_op jit(solution)/shard_map/all_gather | solution.py:12
  366.9 160.2 %while.28 = (s32[]{:T(128)}, f32[8,128,128]{2,1,0:T(8,128)S(1)}, s32[]{:T(128)}, f32[128,8,128,128]{3,2,1,0:T(8,128)}, s32[]{:T(128)}, /*index=5*/s32[]{:T(128)}) while((s32[]{:T(128)}, f32[8,128,128]{2,1,0:T(8,128)S(1)}, s32[]{:T(128)}, f32[128,8,128,128]{3,2,1,0:T(8,128)}, s32[]{:T(128)}, /*index=5*/s32[]{:T(128)}) %tuple.60), condition=%wide.region_2.3_spmd.clone, body=%wide.region_1.2_spmd.clone.sunk | while | flops 393220 | bytes 1572957 | solution.py:20
  368.1 1.2 add_select_fusion.4
  369.4 1.2 add_select_fusion.4
  370.6 1.2 add_select_fusion.4
  371.9 1.2 add_select_fusion.4
  373.1 1.2 add_select_fusion.4
  379.4 1.3 add_select_fusion.4
  380.7 1.3 add_select_fusion.4
  382.0 1.2 add_select_fusion.4
  384.5 1.2 add_select_fusion.4
  398.2 1.2 add_select_fusion.4
  408.3 1.2 add_select_fusion.4
  422.0 1.2 add_select_fusion.4
  432.0 1.2 add_select_fusion.4
  445.8 1.2 add_select_fusion.4
  455.8 1.2 add_select_fusion.4
  469.6 1.2 add_select_fusion.4
  479.6 1.2 add_select_fusion.4
  493.3 1.2 add_select_fusion.4
  503.3 1.2 add_select_fusion.4
  517.1 1.2 add_select_fusion.4
  528.0 1.7 convolution_bitcast_fusion
  529.7 3.2 while.29
  529.7 1.6 add_select_fusion.5
  531.3 1.6 add_select_fusion.5
  532.9 9.7 %all-gather.6.cloned.1.call-done = f32[16,128,128]{2,1,0:T(8,128)} async-done(((f32[8,128,128]{2,1,0:T(8,128)}), f32[16,128,128]{2,1,0:T(8,128)}) %all-gather.6.cloned.1.call-update) | async-done | bytes 1048592 | tf_op jit(solution)/shard_map/all_gather | solution.py:37
  542.6 1.7 fusion.9
  544.4 1.8 multiply_reduce_fusion
  (127 shorter events, 135.3 us)
Async XLA Ops:
  6.5 521.4 %copy-start = (bf16[128,2048]{1,0:T(8,128)(2,1)S(1)}, bf16[128,2048]{1,0:T(8,128)(2,1)}, u32[]{:S(2)}) copy-start(bf16[128,2048]{1,0:T(8,128)(2,1)} %param.7) | copy-start | bytes 1572868
  6.5 18.5 %reduce-scatter.2.cloned.1.call-start = ((), (), s32[]{:S(2)}) async-start(), calls=%async_computation.1 | async-start | bytes 1572864 | tf_op jit(solution)/shard_map/reduce_scatter | solution.py:35
  10.3 356.6 %all-gather.8.cloned.1.call-start = ((), (), s32[]{:S(2)}) async-start(), calls=%async_computation.3 | async-start | bytes 67633152 | tf_op jit(solution)/shard_map/all_gather | solution.py:12
  25.1 504.6 %all-gather.10.cloned.1.call-start = ((), (), s32[]{:S(2)}) async-start(), calls=%async_computation.4 | async-start | bytes 3145728 | tf_op jit(solution)/shard_map/all_gather | solution.py:12
  25.8 516.8 %all-gather.6.cloned.1.call-start = ((), (), s32[]{:S(2)}) async-start(), calls=%async_computation.2 | async-start | bytes 1572864 | tf_op jit(solution)/shard_map/all_gather | solution.py:37
  527.1 0.8 copy-start.1
Sparse Core Ops, SparseCore 0:
  10.4 14.6 reduce-scatter.1
  28.8 338.0 all-gather.7
  368.7 16.1 all-gather.9
  528.0 14.5 all-gather.5
where the time goes:
time: 564 us; the launch traced here: 554 us
  waiting for transfers between devices  366 us (65%)
  other arithmetic  160 us (28%)
  between operations  13.2 us (2%)
  matrix products  7.55 us (1%)
    all_gather x2, waiting for transfers between devices, carried_in(): everything = lax.all_gather(value, axis)  341 us
    select_n x130, other arithmetic, step(): return jnp.where(reached, new, before)  160 us
    reduce_scatter x1, waiting for transfers between devices, shards(): lax.psum_scatter(own_state, 'narrow', scatter_dimension=0, tiled=True)  14.7 us
  transfers between devices with their start and end apart: 4, of which 3 were waited for; matrix products, arithmetic and copies ran while one was open for 29% of the time, Pallas kernels for 0%

commit v1 on v0

v1 whole, which is shorter than its diff:
```python
import functools

import jax
import jax.numpy as jnp
from jax import lax
from jax.experimental import pallas as pl
from jax.experimental.pallas import tpu as pltpu
from jax.sharding import PartitionSpec as P

HEADS = 16
DIM = 128
GROUP = HEADS // 2
CHUNKS = 4
PER = GROUP // CHUNKS
ROWS = PER * DIM
NX, NY, NZ = 4, 4, 8
PLANE = NX * NY
SLICE = ROWS // PLANE
MESH = pl.DeviceIdType.MESH


def dot(a, b, dims):
    return lax.dot_general(a, b, (dims, ((), ())), preferred_element_type=jnp.float32)


def kernel(q_ref, k_ref, v_ref, o_ref, own, part, total, up, prefix, plane, zrecv, down, carry, give, other, local,
           ex_send, ex_recv, up_send, up_recv, z_send, z_recv, dn_send, dn_recv, fx_send, fx_recv):
    wide, core = lax.axis_index("wide"), lax.axis_index("narrow")
    here = wide % PLANE
    z = wide // PLANE
    partner = (wide, 1 - core)

    def chip_in_plane(i):
        return z * PLANE + i

    def remote(src, dst, send, recv, to):
        return pltpu.make_async_remote_copy(src, dst, send, recv, device_id=to, device_id_type=MESH)

    def arrived(ref, sem):
        pltpu.make_async_copy(ref, ref, sem).wait()

    barrier = pltpu.get_barrier_semaphore()
    pl.semaphore_signal(barrier, inc=1, device_id=partner, device_id_type=MESH)
    for i in range(1, PLANE):
        pl.semaphore_signal(barrier, inc=1, device_id=(chip_in_plane((here + i) % PLANE), core), device_id_type=MESH)
    for i in range(1, NZ):
        pl.semaphore_signal(barrier, inc=1, device_id=(((z + i) % NZ) * PLANE + here, core), device_id_type=MESH)

    def columns(group, head):
        return pl.ds(pl.multiple_of(group * (GROUP * DIM) + head * DIM, DIM), DIM)

    def states(group):
        for head in range(GROUP):
            at = columns(group, head)
            own[group, head // PER, pl.ds((head % PER) * DIM, DIM), :] = dot(k_ref[:, at], v_ref[:, at], ((0,), (0,)))

    states(1 - core)
    pl.semaphore_wait(barrier, PLANE - 1 + NZ - 1 + 1)
    for k in range(CHUNKS):
        remote(own.at[1 - core, k], part.at[k], ex_send.at[k], ex_recv.at[k], partner).start()
    states(core)

    for k in range(CHUNKS):
        arrived(part.at[k], ex_recv.at[k])
        summed = own[core, k] + part[k]
        total[k] = summed.reshape(PLANE, SLICE, DIM)
        up[k, here] = total[k, here]
        for i in range(1, PLANE):
            root = (here + i) % PLANE
            remote(total.at[k, root], up.at[k, here], up_send.at[k], up_recv.at[k], (chip_in_plane(root), core)).start()

    rows = lax.broadcasted_iota(jnp.int32, (DIM, DIM), 0)
    cols = lax.broadcasted_iota(jnp.int32, (DIM, DIM), 1)
    causal = rows >= cols
    for head in range(HEADS):
        at = pl.ds(head * DIM, DIM)
        scores = dot(q_ref[:, at], k_ref[:, at], ((1,), (1,)))
        scores = jnp.where(causal, scores, 0.0).astype(jnp.bfloat16)
        local[:, at] = dot(scores, v_ref[:, at], ((1,), (0,)))

    for k in range(CHUNKS):
        arrived(up.at[k, pl.ds(0, PLANE - 1)], up_recv.at[k])
        before = jnp.zeros((SLICE, DIM), jnp.float32)
        for i in range(PLANE):
            prefix[k, i] = before
            before = before + up[k, i]
        plane[k] = before

        @pl.loop(z + 1, NZ)
        def _(to):
            remote(plane.at[k], zrecv.at[k, z], z_send.at[k, to], z_recv.at[k, z], (to * PLANE + here, core)).start()

    for k in range(CHUNKS):
        def add(frm, acc):
            arrived(zrecv.at[k, frm], z_recv.at[k, frm])
            return acc + zrecv[k, frm]

        below = lax.fori_loop(0, z, add, jnp.zeros((SLICE, DIM), jnp.float32))
        down[k] = prefix[k] + below[None]
        carry[k, here] = down[k, here]
        for i in range(1, PLANE):
            chip = (here + i) % PLANE
            remote(down.at[k, chip], carry.at[k, here], dn_send.at[k], dn_recv.at[k], (chip_in_plane(chip), core)).start()

    def finish(group, head, state):
        at = columns(group, head)
        high = state.astype(jnp.bfloat16)
        low = (state - high.astype(jnp.float32)).astype(jnp.bfloat16)
        q = q_ref[:, at]
        whole = local[:, at] + (dot(q, high, ((1,), (0,))) + dot(q, low, ((1,), (0,))))
        factor = lax.rsqrt(jnp.mean(whole * whole, axis=-1, keepdims=True) + 1e-05)
        o_ref[:, at] = (whole * factor).astype(jnp.bfloat16)

    for k in range(CHUNKS):
        arrived(carry.at[k, pl.ds(0, PLANE - 1)], dn_recv.at[k])
        chip_carry = carry[k].reshape(ROWS, DIM)
        give[k] = chip_carry + jnp.where(core == 0, own[core, k], 0.0)
        remote(give.at[k], other.at[k], fx_send.at[k], fx_recv.at[k], partner).start()
        mine = chip_carry + jnp.where(core == 0, 0.0, part[k])
        for j in range(PER):
            finish(core, k * PER + j, mine[j * DIM:(j + 1) * DIM])

    for k in range(CHUNKS):
        arrived(other.at[k], fx_recv.at[k])
        for j in range(PER):
            finish(1 - core, k * PER + j, other[k, pl.ds(j * DIM, DIM), :])

    for k in range(CHUNKS):
        arrived(own.at[1 - core, k], ex_send.at[k])
        arrived(total.at[k, pl.ds(0, PLANE - 1)], up_send.at[k])
        arrived(down.at[k, pl.ds(0, PLANE - 1)], dn_send.at[k])
        arrived(give.at[k], fx_send.at[k])

        @pl.loop(z + 1, NZ)
        def _(to):
            arrived(plane.at[k], z_send.at[k, to])


def shards(queries, keys, values):
    f32 = jnp.float32
    dma = pltpu.SemaphoreType.DMA
    vmem = pl.BlockSpec(memory_space=pltpu.VMEM)
    return pl.pallas_call(
        kernel,
        out_shape=jax.ShapeDtypeStruct(queries.shape, queries.dtype),
        in_specs=[vmem] * 3,
        out_specs=vmem,
        scratch_shapes=[
            pltpu.VMEM((2, CHUNKS, ROWS, DIM), f32),
            pltpu.VMEM((CHUNKS, ROWS, DIM), f32),
            pltpu.VMEM((CHUNKS, PLANE, SLICE, DIM), f32),
            pltpu.VMEM((CHUNKS, PLANE, SLICE, DIM), f32),
            pltpu.VMEM((CHUNKS, PLANE, SLICE, DIM), f32),
            pltpu.VMEM((CHUNKS, SLICE, DIM), f32),
            pltpu.VMEM((CHUNKS, NZ, SLICE, DIM), f32),
            pltpu.VMEM((CHUNKS, PLANE, SLICE, DIM), f32),
            pltpu.VMEM((CHUNKS, PLANE, SLICE, DIM), f32),
            pltpu.VMEM((CHUNKS, ROWS, DIM), f32),
            pltpu.VMEM((CHUNKS, ROWS, DIM), f32),
            pltpu.VMEM((DIM, HEADS * DIM), f32),
            dma((CHUNKS,)), dma((CHUNKS,)), dma((CHUNKS,)), dma((CHUNKS,)),
            dma((CHUNKS, NZ)), dma((CHUNKS, NZ)),
            dma((CHUNKS,)), dma((CHUNKS,)), dma((CHUNKS,)), dma((CHUNKS,)),
        ],
        compiler_params=pltpu.CompilerParams(collective_id=0, has_side_effects=True),
        name="prefix_attention",
    )(queries, keys, values)


def solution(mesh):
    placed = P(("wide", "narrow"), None)
    return jax.shard_map(shards, mesh=mesh, in_specs=(placed,) * 3, out_specs=placed, check_vma=False)
```

time: 564 us -> 36.3 us (0.06)
  the two profiles are of different devices: /device:TPU:225 before, /device:TPU:1 now
where the time goes in v1:
time: 36.3 us; the launch traced here: 36.2 us
  Pallas kernels  34.3 us (94%)
  local copies, waits for them, and re-layouts  1.88 us (5%)
    pallas_call x1, Pallas kernels, shards(): pl.pallas_call(kernel, out_shape=jax.ShapeDtypeStruct(queries.shape, quer...  34.3 us
    unnamed x1, local copies, waits for them, and re-layouts  1.88 us

profile of v1, /device:TPU:1, one launch (start us, length us, event | category | flops | bytes accessed | tf_op | source)
XLA Modules:
  0.0 36.2 jit_solution(16879471581019621820)
XLA Ops:
  0.0 34.3 %prefix_attention.1 = bf16[128,2048]{1,0:T(8,128)(2,1)} custom-call(bf16[128,2048]{1,0:T(8,128)(2,1)} %q_ref.1, bf16[128,2048]{1,0:T(8,128)(2,1)} %k_ref.1, bf16[128,2048]{1,0:T(8,128)(2,1)} %v_ref.1), custom_call_target="tpu_custom_call" | custom-call | tf_op jit(solution)/shard_map/prefix_attention/pallas_call | solution.py:143
  34.3 1.9 %copy.5 = bf16[128,2048]{1,0:T(8,128)(2,1)} copy(bf16[128,2048]{1,0:T(8,128)(2,1)} %prefix_attention.1) | data formatting | bytes 1048576

commit v2 on v0

v2 whole, which is shorter than its diff:
```python
import contextlib

import jax
import jax.numpy as jnp
from jax import lax
from jax.experimental import pallas as pl
from jax.experimental.pallas import tpu as pltpu
from jax.sharding import PartitionSpec as P

HEADS = 16
DIM = 128
GROUP = HEADS // 2
CHUNKS = ((0, 2), (2, 2), (4, 2), (6, 1), (7, 1))
N = len(CHUNKS)
NZ = 8
HALF = NZ // 2
PLANE = 16
PIECE = DIM // PLANE
LAGS = (0, 1, 1, 1, 1, 1, 2, 2)
MESH = pl.DeviceIdType.MESH


def scope(name):
    return contextlib.nullcontext()


def dot(a, b, dims):
    return lax.dot_general(a, b, (dims, ((), ())), preferred_element_type=jnp.float32)


def kernel(q_hbm, k_hbm, v_hbm, o_ref, q_ref, k_ref, v_ref, own, part, total, up, prefix, plane, below, zrecv, down,
           carry, give, other, local, in_sem, hello, go,
           ex_send, ex_recv, up_send, up_recv, z_send, z_recv, dn_send, dn_recv, fx_send, fx_recv):
    wide, core = lax.axis_index("wide"), lax.axis_index("narrow")
    here = wide % PLANE
    z = wide // PLANE
    partner = (wide, 1 - core)
    z_first = jnp.where(z < HALF, 0, HALF - 1)
    z_last = jnp.where(z < HALF, HALF, NZ)

    def chip_in_plane(i):
        return z * PLANE + i

    def remote(src, dst, send, recv, to):
        return pltpu.make_async_remote_copy(src, dst, send, recv, device_id=to, device_id_type=MESH)

    def arrived(ref, sem):
        pltpu.make_async_copy(ref, ref, sem).wait()

    def rows(k):
        first, count = CHUNKS[k]
        return pl.ds(first * DIM, count * DIM)

    def slice_of(k, i):
        first, count = CHUNKS[k]
        return pl.ds(pl.multiple_of(first * DIM + i * (count * PIECE), 8), count * PIECE)

    def root_rows(k):
        first, count = CHUNKS[k]
        return pl.ds(first * PIECE, count * PIECE)

    def all_but_one(k):
        first, count = CHUNKS[k]
        return pl.ds(first * DIM, (PLANE - 1) * count * PIECE)

    with scope("a_sig"):
        barrier = pltpu.get_barrier_semaphore()

        @pl.when(core == 0)
        def _():
            pl.semaphore_signal(barrier, inc=1, device_id=partner, device_id_type=MESH)

        for i in range(1, PLANE):
            pl.semaphore_signal(barrier, inc=1, device_id=(chip_in_plane((here + i) % PLANE), 0), device_id_type=MESH)

        @pl.loop(z_first, z)
        def _(frm):
            pl.semaphore_signal(barrier, inc=1, device_id=(frm * PLANE + here, 0), device_id_type=MESH)

        loads = [pltpu.make_async_copy(src, dst, in_sem.at[i])
                 for i, (src, dst) in enumerate(((k_hbm, k_ref), (v_hbm, v_ref), (q_hbm, q_ref)))]
        for load in loads:
            load.start()

        @pl.when(core == 1)
        def _():
            pl.semaphore_wait(barrier, 1)
            pl.semaphore_signal(hello, inc=1, device_id=partner, device_id_type=MESH)

        @pl.when(core == 0)
        def _():
            pl.semaphore_wait(hello, 1)

    def columns(group, head, count=1):
        return pl.ds(pl.multiple_of(group * (GROUP * DIM) + head * DIM, DIM), count * DIM)

    def states(group, k):
        first, count = CHUNKS[k]
        for head in range(first, first + count):
            at = columns(group, head)
            own[group, pl.ds(head * DIM, DIM), :] = dot(k_ref[:, at], v_ref[:, at], ((0,), (0,)))

    with scope("b_load"):
        loads[0].wait()
        loads[1].wait()
    with scope("b_states"):
        for k in range(N):
            states(1 - core, k)
            remote(own.at[1 - core, rows(k)], part.at[rows(k)], ex_send.at[k], ex_recv.at[k], partner).start()
        for k in range(N):
            states(core, k)
    with scope("c_barrier"):
        @pl.when(core == 0)
        def _():
            z_peers = jnp.where(z == HALF - 1, HALF, z_last - 1 - z)
            pl.semaphore_wait(barrier, 2 * (PLANE - 1 + z_peers))
            pl.semaphore_signal(go, inc=1, device_id=partner, device_id_type=MESH)

        @pl.when(core == 1)
        def _():
            pl.semaphore_wait(go, 1)

    for k in range(N):
        with scope(f"f_exwait{k}"):
            arrived(part.at[rows(k)], ex_recv.at[k])
        with scope(f"f_up{k}"):
            total[rows(k)] = own[core, rows(k)] + part[rows(k)]
            up[slice_of(k, here)] = total[slice_of(k, here)]
            for i in range(1, PLANE):
                root = (here + i) % PLANE
                remote(total.at[slice_of(k, root)], up.at[slice_of(k, here)], up_send.at[k], up_recv.at[k],
                       (chip_in_plane(root), core)).start()

    with scope("g_local"):
        loads[2].wait()
        causal = lax.broadcasted_iota(jnp.int32, (DIM, DIM), 0) >= lax.broadcasted_iota(jnp.int32, (DIM, DIM), 1)
        for head in range(HEADS):
            at = pl.ds(head * DIM, DIM)
            scores = dot(q_ref[:, at], k_ref[:, at], ((1,), (1,)))
            scores = jnp.where(causal, scores, 0.0).astype(jnp.bfloat16)
            local[:, at] = dot(scores, v_ref[:, at], ((1,), (0,)))

    def to_plane(source, k, to):
        return remote(source.at[root_rows(k)], zrecv.at[z, root_rows(k)], z_send.at[k, to], z_recv.at[k, z],
                      (to * PLANE + here, core))

    def root(k):
        with scope(f"h_upwait{k}"):
            arrived(up.at[all_but_one(k)], up_recv.at[k])
        with scope(f"h_root{k}"):
            before = jnp.zeros((CHUNKS[k][1] * PIECE, DIM), jnp.float32)
            for i in range(PLANE):
                prefix[slice_of(k, i)] = before
                before = before + up[slice_of(k, i)]
            plane[root_rows(k)] = before

            @pl.loop(z + 1, z_last)
            def _(to):
                to_plane(plane, k, to).start()

    def carries(k):
        def add(frm, acc):
            arrived(zrecv.at[frm, root_rows(k)], z_recv.at[k, frm])
            return acc + zrecv[frm, root_rows(k)]

        with scope(f"i_zwait{k}"):
            earlier = lax.fori_loop(z_first, z, add, jnp.zeros((CHUNKS[k][1] * PIECE, DIM), jnp.float32))

        with scope(f"i_down{k}"):
            @pl.when(z == HALF - 1)
            def _():
                below[root_rows(k)] = earlier + plane[root_rows(k)]
                for to in range(HALF, NZ):
                    to_plane(below, k, to).start()

            for i in range(PLANE):
                down[slice_of(k, i)] = prefix[slice_of(k, i)] + earlier
            carry[slice_of(k, here)] = down[slice_of(k, here)]
            for i in range(1, PLANE):
                chip = (here + i) % PLANE
                remote(down.at[slice_of(k, chip)], carry.at[slice_of(k, here)], dn_send.at[k], dn_recv.at[k],
                       (chip_in_plane(chip), core)).start()

    for step in range(N + max(LAGS)):
        if step < N:
            root(step)
        for lag in sorted(set(LAGS)):
            if 0 <= step - lag < N:
                wanted = [i for i in range(NZ) if LAGS[i] == lag]

                @pl.when((z >= wanted[0]) & (z <= wanted[-1]))
                def _():
                    carries(step - lag)

    def finish(group, head, state):
        at = columns(group, head)
        high = state.astype(jnp.bfloat16)
        low = (state - high.astype(jnp.float32)).astype(jnp.bfloat16)
        q = q_ref[:, at]
        whole = local[:, at] + (dot(q, high, ((1,), (0,))) + dot(q, low, ((1,), (0,))))
        factor = lax.rsqrt(jnp.mean(whole * whole, axis=-1, keepdims=True) + 1e-05)
        o_ref[:, at] = (whole * factor).astype(jnp.bfloat16)

    def finish_other(k):
        with scope(f"k_fxwait{k}"):
            arrived(other.at[rows(k)], fx_recv.at[k])
        with scope(f"k_fin{k}"):
            first, count = CHUNKS[k]
            for head in range(first, first + count):
                finish(1 - core, head, other[pl.ds(head * DIM, DIM)])

    for k in range(N):
        with scope(f"j_dnwait{k}"):
            arrived(carry.at[all_but_one(k)], dn_recv.at[k])
        with scope(f"j_fin{k}"):
            give[rows(k)] = carry[rows(k)] + jnp.where(core == 0, own[core, rows(k)], 0.0)
            remote(give.at[rows(k)], other.at[rows(k)], fx_send.at[k], fx_recv.at[k], partner).start()
            first, count = CHUNKS[k]
            for head in range(first, first + count):
                at = pl.ds(head * DIM, DIM)
                finish(core, head, carry[at] + jnp.where(core == 0, 0.0, part[at]))
        if k:
            finish_other(k - 1)
    finish_other(N - 1)

    with scope("l_waits"):
        for k in range(N):
            arrived(own.at[1 - core, rows(k)], ex_send.at[k])
            arrived(total.at[all_but_one(k)], up_send.at[k])
            arrived(down.at[all_but_one(k)], dn_send.at[k])
            arrived(give.at[rows(k)], fx_send.at[k])

            @pl.loop(z + 1, z_last)
            def _(to):
                arrived(plane.at[root_rows(k)], z_send.at[k, to])

            @pl.when(z == HALF - 1)
            def _():
                for to in range(HALF, NZ):
                    arrived(below.at[root_rows(k)], z_send.at[k, to])


def shards(queries, keys, values):
    dma = pltpu.SemaphoreType.DMA
    hbm = pl.BlockSpec(memory_space=pltpu.HBM)
    block = pltpu.VMEM(queries.shape, queries.dtype)
    state = pltpu.VMEM((GROUP * DIM, DIM), jnp.float32)
    root = pltpu.VMEM((GROUP * PIECE, DIM), jnp.float32)
    return pl.pallas_call(
        kernel,
        out_shape=pltpu.VMEM(queries.shape, queries.dtype),
        in_specs=[hbm] * 3,
        out_specs=pl.BlockSpec(memory_space=pltpu.VMEM),
        scratch_shapes=[
            block, block, block,
            pltpu.VMEM((2, GROUP * DIM, DIM), jnp.float32),
            state, state, state, state, root, root,
            pltpu.VMEM((NZ, GROUP * PIECE, DIM), jnp.float32),
            state, state, state, state,
            pltpu.VMEM((DIM, HEADS * DIM), jnp.float32),
            dma((3,)), pltpu.SemaphoreType.REGULAR, pltpu.SemaphoreType.REGULAR,
            dma((N,)), dma((N,)), dma((N,)), dma((N,)),
            dma((N, NZ)), dma((N, NZ)),
            dma((N,)), dma((N,)), dma((N,)), dma((N,)),
        ],
        compiler_params=pltpu.CompilerParams(collective_id=0, has_side_effects=True),
        name="prefix_attention",
    )(*(pltpu.with_memory_space_constraint(x, pltpu.HBM) for x in (queries, keys, values)))


def solution(mesh):
    placed = P(("wide", "narrow"), None)
    return jax.shard_map(shards, mesh=mesh, in_specs=(placed,) * 3, out_specs=placed, check_vma=False)
```

time: 564 us -> 29.9 us (0.05); the launches traced: 554 us -> 29.8 us
  waiting for transfers between devices: 366 us -> 0 us
  other arithmetic: 160 us -> 0 us
  Pallas kernels: 0 us -> 29 us
  between operations: 13.2 us -> 0.01 us
  matrix products: 7.55 us -> 0 us
    all_gather x3 -> x0, waiting for transfers between devices: 351 us -> none  [the longest x2 341 us: carried_in(): everything = lax.all_gather(value, axis)]
    select_n x130 -> x0, other arithmetic: 160 us -> none  [step(): return jnp.where(reached, new, before)]
    pallas_call x0 -> x1, Pallas kernels: none -> 29 us  [shards(): pl.pallas_call(kernel, out_shape=pltpu.VMEM(queries.shape, queries.dtype)...]
    reduce_scatter x1 -> x0, waiting for transfers between devices: 14.7 us -> none  [shards(): lax.psum_scatter(own_state, 'narrow', scatter_dimension=0, tiled=True)]
    dot_general x4 -> x0, matrix products: 7.55 us -> none  [the longest x1 2.34 us: shards(): jnp.einsum('shd,she->hde', k_heads, v_heads, preferred_element_type=jnp.f...]
  transfers between devices with their start and end apart: 4 -> 0, of which waited for: 3 -> 0; matrix products, arithmetic and copies ran while one was open for 29% -> 0% of each run, Pallas kernels for 0% -> 0%
where the time goes in v2:
time: 29.9 us; the launch traced here: 29.8 us
  Pallas kernels  29 us (97%)
  local copies, waits for them, and re-layouts  0.8 us (3%)
    pallas_call x1, Pallas kernels, shards(): pl.pallas_call(kernel, out_shape=pltpu.VMEM(queries.shape, queries.dtype)...  29 us
    unnamed x1, local copies, waits for them, and re-layouts  0.8 us

profile of v2, /device:TPU:225, one launch (start us, length us, event | category | flops | bytes accessed | tf_op | source)
XLA Modules:
  0.0 29.8 jit_solution(13565779163580037527)
XLA Ops:
  0.0 29.0 %prefix_attention.1 = bf16[128,2048]{1,0:T(8,128)(2,1)S(1)} custom-call(bf16[128,2048]{1,0:T(8,128)(2,1)} %q_hbm.1, bf16[128,2048]{1,0:T(8,128)(2,1)} %k_hbm.1, bf16[128,2048]{1,0:T(8,128)(2,1)} %v_hbm.1), custom_call_target="tpu_custom_call" | custom-call | tf_op jit(solution)/shard_map/prefix_attention/pallas_call | solution.py:249
  29.1 0.8 %copy.5 = bf16[128,2048]{1,0:T(8,128)(2,1)} copy(bf16[128,2048]{1,0:T(8,128)(2,1)S(1)} %prefix_attention.1) | data formatting | bytes 1048576

commit v3 on v2

--- a/solution.py
+++ b/solution.py
@@ -1,4 +1,5 @@
 import contextlib
+import functools
 
 import jax
 import jax.numpy as jnp
@@ -16,7 +17,7 @@
 HALF = NZ // 2
 PLANE = 16
 PIECE = DIM // PLANE
-LAGS = (0, 1, 1, 1, 1, 1, 2, 2)
+LAGS = (0, 1, 1, 2, 3, 3, 3, 3)
 MESH = pl.DeviceIdType.MESH
 
 
@@ -28,15 +29,15 @@
     return lax.dot_general(a, b, (dims, ((), ())), preferred_element_type=jnp.float32)
 
 
-def kernel(q_hbm, k_hbm, v_hbm, o_ref, q_ref, k_ref, v_ref, own, part, total, up, prefix, plane, below, zrecv, down,
+def kernel(q_hbm, k_hbm, v_hbm, o_ref, q_ref, k_ref, v_ref, own, part, total, up, prefix, plane, below, pair, zrecv, down,
            carry, give, other, local, in_sem, hello, go,
            ex_send, ex_recv, up_send, up_recv, z_send, z_recv, dn_send, dn_recv, fx_send, fx_recv):
     wide, core = lax.axis_index("wide"), lax.axis_index("narrow")
     here = wide % PLANE
     z = wide // PLANE
     partner = (wide, 1 - core)
-    z_first = jnp.where(z < HALF, 0, HALF - 1)
-    z_last = jnp.where(z < HALF, HALF, NZ)
+    z_first = jnp.where(z < HALF, 0, 1)
+    z_last = jnp.where(z < 2, HALF, NZ)
 
     def chip_in_plane(i):
         return z * PLANE + i
@@ -65,8 +66,9 @@
 
     with scope("a_sig"):
         barrier = pltpu.get_barrier_semaphore()
-
-        @pl.when(core == 0)
+        late = (z < HALF) | ((z < NZ - 1) & (here % 4 >= 2) & (here >= PLANE // 2))
+
+        @pl.when(jnp.where(late, 1, 0) == core)
         def _():
             pl.semaphore_signal(barrier, inc=1, device_id=partner, device_id_type=MESH)
 
@@ -75,21 +77,38 @@
 
         @pl.loop(z_first, z)
         def _(frm):
-            pl.semaphore_signal(barrier, inc=1, device_id=(frm * PLANE + here, 0), device_id_type=MESH)
+            pl.semaphore_signal(barrier, inc=1, device_id=(frm * PLANE + here, 1), device_id_type=MESH)
 
         loads = [pltpu.make_async_copy(src, dst, in_sem.at[i])
                  for i, (src, dst) in enumerate(((k_hbm, k_ref), (v_hbm, v_ref), (q_hbm, q_ref)))]
         for load in loads:
             load.start()
 
+    z_peers = 2 * (z_last - 1 - z + jnp.where(z == 1, NZ - HALF, 0))
+
+    def meet_above(count):
         @pl.when(core == 1)
         def _():
-            pl.semaphore_wait(barrier, 1)
+            pl.semaphore_wait(barrier, count)
             pl.semaphore_signal(hello, inc=1, device_id=partner, device_id_type=MESH)
 
         @pl.when(core == 0)
         def _():
             pl.semaphore_wait(hello, 1)
+
+    def meet_plane(count):
+        @pl.when(core == 0)
+        def _():
+            pl.semaphore_wait(barrier, count)
+            pl.semaphore_signal(go, inc=1, device_id=partner, device_id_type=MESH)
+
+        @pl.when(core == 1)
+        def _():
+            pl.semaphore_wait(go, 1)
+
+    def exchange():
+        for k in range(N):
+            remote(own.at[1 - core, rows(k)], part.at[rows(k)], ex_send, ex_recv.at[min(k, 1)], partner).start()
 
     def columns(group, head, count=1):
         return pl.ds(pl.multiple_of(group * (GROUP * DIM) + head * DIM, DIM), count * DIM)
@@ -106,29 +125,30 @@
     with scope("b_states"):
         for k in range(N):
             states(1 - core, k)
-            remote(own.at[1 - core, rows(k)], part.at[rows(k)], ex_send.at[k], ex_recv.at[k], partner).start()
-        for k in range(N):
             states(core, k)
     with scope("c_barrier"):
-        @pl.when(core == 0)
-        def _():
-            z_peers = jnp.where(z == HALF - 1, HALF, z_last - 1 - z)
-            pl.semaphore_wait(barrier, 2 * (PLANE - 1 + z_peers))
-            pl.semaphore_signal(go, inc=1, device_id=partner, device_id_type=MESH)
-
-        @pl.when(core == 1)
-        def _():
-            pl.semaphore_wait(go, 1)
+        @pl.when(jnp.logical_not(late))
+        def _():
+            meet_above(z_peers + 1)
+            exchange()
+            meet_plane(2 * (PLANE - 1))
+
+        @pl.when(late)
+        def _():
+            meet_plane(2 * (PLANE - 1) + 1)
+            exchange()
 
     for k in range(N):
         with scope(f"f_exwait{k}"):
-            arrived(part.at[rows(k)], ex_recv.at[k])
+            if k < 2:
+                rest = GROUP - CHUNKS[k][0] if k else CHUNKS[0][1]
+                arrived(part.at[pl.ds(CHUNKS[k][0] * DIM, rest * DIM)], ex_recv.at[k])
         with scope(f"f_up{k}"):
             total[rows(k)] = own[core, rows(k)] + part[rows(k)]
             up[slice_of(k, here)] = total[slice_of(k, here)]
             for i in range(1, PLANE):
                 root = (here + i) % PLANE
-                remote(total.at[slice_of(k, root)], up.at[slice_of(k, here)], up_send.at[k], up_recv.at[k],
+                remote(total.at[slice_of(k, root)], up.at[slice_of(k, here)], up_send, up_recv.at[k],
                        (chip_in_plane(root), core)).start()
 
     with scope("g_local"):
@@ -140,8 +160,13 @@
             scores = jnp.where(causal, scores, 0.0).astype(jnp.bfloat16)
             local[:, at] = dot(scores, v_ref[:, at], ((1,), (0,)))
 
+    with scope("g_meet"):
+        @pl.when(late)
+        def _():
+            meet_above(z_peers)
+
     def to_plane(source, k, to):
-        return remote(source.at[root_rows(k)], zrecv.at[z, root_rows(k)], z_send.at[k, to], z_recv.at[k, z],
+        return remote(source.at[root_rows(k)], zrecv.at[z, root_rows(k)], z_send, z_recv.at[k],
                       (to * PLANE + here, core))
 
     def root(k):
@@ -158,27 +183,33 @@
             def _(to):
                 to_plane(plane, k, to).start()
 
+    def planes_arrived(count, at, sem):
+        for n in range(1, NZ - 1):
+            @pl.when(count == n)
+            def _():
+                arrived(zrecv.at[pl.ds(0, n), at], sem)
+
+    def earlier(k):
+        with scope(f"i_zwait{k}"):
+            planes_arrived(z - z_first, root_rows(k), z_recv.at[k])
+            below[root_rows(k)] = lax.fori_loop(z_first, z, lambda frm, acc: acc + zrecv[frm, root_rows(k)],
+                                                jnp.zeros((CHUNKS[k][1] * PIECE, DIM), jnp.float32))
+
+        @pl.when(z == 1)
+        def _():
+            pair[root_rows(k)] = below[root_rows(k)] + plane[root_rows(k)]
+            for to in range(HALF, NZ):
+                to_plane(pair, k, to).start()
+
     def carries(k):
-        def add(frm, acc):
-            arrived(zrecv.at[frm, root_rows(k)], z_recv.at[k, frm])
-            return acc + zrecv[frm, root_rows(k)]
-
-        with scope(f"i_zwait{k}"):
-            earlier = lax.fori_loop(z_first, z, add, jnp.zeros((CHUNKS[k][1] * PIECE, DIM), jnp.float32))
-
         with scope(f"i_down{k}"):
-            @pl.when(z == HALF - 1)
-            def _():
-                below[root_rows(k)] = earlier + plane[root_rows(k)]
-                for to in range(HALF, NZ):
-                    to_plane(below, k, to).start()
-
+            above = below[root_rows(k)]
             for i in range(PLANE):
-                down[slice_of(k, i)] = prefix[slice_of(k, i)] + earlier
+                down[slice_of(k, i)] = prefix[slice_of(k, i)] + above
             carry[slice_of(k, here)] = down[slice_of(k, here)]
             for i in range(1, PLANE):
                 chip = (here + i) % PLANE
-                remote(down.at[slice_of(k, chip)], carry.at[slice_of(k, here)], dn_send.at[k], dn_recv.at[k],
+                remote(down.at[slice_of(k, chip)], carry.at[slice_of(k, here)], dn_send, dn_recv.at[k],
                        (chip_in_plane(chip), core)).start()
 
     for step in range(N + max(LAGS)):
@@ -188,8 +219,9 @@
             if 0 <= step - lag < N:
                 wanted = [i for i in range(NZ) if LAGS[i] == lag]
 
-                @pl.when((z >= wanted[0]) & (z <= wanted[-1]))
+                @pl.when(functools.reduce(jnp.logical_or, [z == i for i in wanted]))
                 def _():
+                    earlier(step - lag)
                     carries(step - lag)
 
     def finish(group, head, state):
@@ -214,7 +246,7 @@
             arrived(carry.at[all_but_one(k)], dn_recv.at[k])
         with scope(f"j_fin{k}"):
             give[rows(k)] = carry[rows(k)] + jnp.where(core == 0, own[core, rows(k)], 0.0)
-            remote(give.at[rows(k)], other.at[rows(k)], fx_send.at[k], fx_recv.at[k], partner).start()
+            remote(give.at[rows(k)], other.at[rows(k)], fx_send, fx_recv.at[k], partner).start()
             first, count = CHUNKS[k]
             for head in range(first, first + count):
                 at = pl.ds(head * DIM, DIM)
@@ -224,20 +256,11 @@
     finish_other(N - 1)
 
     with scope("l_waits"):
-        for k in range(N):
-            arrived(own.at[1 - core, rows(k)], ex_send.at[k])
-            arrived(total.at[all_but_one(k)], up_send.at[k])
-            arrived(down.at[all_but_one(k)], dn_send.at[k])
-            arrived(give.at[rows(k)], fx_send.at[k])
-
-            @pl.loop(z + 1, z_last)
-            def _(to):
-                arrived(plane.at[root_rows(k)], z_send.at[k, to])
-
-            @pl.when(z == HALF - 1)
-            def _():
-                for to in range(HALF, NZ):
-                    arrived(below.at[root_rows(k)], z_send.at[k, to])
+        arrived(own.at[1 - core], ex_send)
+        arrived(total.at[pl.ds(0, (PLANE - 1) * GROUP * PIECE)], up_send)
+        arrived(down.at[pl.ds(0, (PLANE - 1) * GROUP * PIECE)], dn_send)
+        arrived(give, fx_send)
+        planes_arrived(z_last - 1 - z + jnp.where(z == 1, NZ - HALF, 0), pl.ds(0, GROUP * PIECE), z_send)
 
 
 def shards(queries, keys, values):
@@ -254,14 +277,12 @@
         scratch_shapes=[
             block, block, block,
             pltpu.VMEM((2, GROUP * DIM, DIM), jnp.float32),
-            state, state, state, state, root, root,
+            state, state, state, state, root, root, root,
             pltpu.VMEM((NZ, GROUP * PIECE, DIM), jnp.float32),
             state, state, state, state,
             pltpu.VMEM((DIM, HEADS * DIM), jnp.float32),
             dma((3,)), pltpu.SemaphoreType.REGULAR, pltpu.SemaphoreType.REGULAR,
-            dma((N,)), dma((N,)), dma((N,)), dma((N,)),
-            dma((N, NZ)), dma((N, NZ)),
-            dma((N,)), dma((N,)), dma((N,)), dma((N,)),
+            dma, dma((2,)), dma, dma((N,)), dma, dma((N,)), dma, dma((N,)), dma, dma((N,)),
         ],
         compiler_params=pltpu.CompilerParams(collective_id=0, has_side_effects=True),
         name="prefix_attention",

time: 29.9 us -> 27.8 us (0.930)
  Pallas kernels: 29 us -> 26.9 us
    pallas_call x1, Pallas kernels: 29 us -> 26.9 us  [shards(): pl.pallas_call(kernel, out_shape=pltpu.VMEM(queries.shape, queries.dtype)...]
where the time goes in v3:
time: 27.8 us; the launch traced here: 27.7 us
  Pallas kernels  26.9 us (97%)
  local copies, waits for them, and re-layouts  0.8 us (3%)
    pallas_call x1, Pallas kernels, shards(): pl.pallas_call(kernel, out_shape=pltpu.VMEM(queries.shape, queries.dtype)...  26.9 us
    unnamed x1, local copies, waits for them, and re-layouts  0.8 us

profile of v3, /device:TPU:225, one launch (start us, length us, event | category | flops | bytes accessed | tf_op | source)
XLA Modules:
  0.0 27.7 jit_solution(8320702717418411239)
XLA Ops:
  0.0 26.9 %prefix_attention.1 = bf16[128,2048]{1,0:T(8,128)(2,1)S(1)} custom-call(bf16[128,2048]{1,0:T(8,128)(2,1)} %q_hbm.1, bf16[128,2048]{1,0:T(8,128)(2,1)} %k_hbm.1, bf16[128,2048]{1,0:T(8,128)(2,1)} %v_hbm.1), custom_call_target="tpu_custom_call" | custom-call | tf_op jit(solution)/shard_map/prefix_attention/pallas_call | solution.py:272
  26.9 0.8 %copy.5 = bf16[128,2048]{1,0:T(8,128)(2,1)} copy(bf16[128,2048]{1,0:T(8,128)(2,1)S(1)} %prefix_attention.1) | data formatting | bytes 1048576

commit v4 on v3

--- a/solution.py
+++ b/solution.py
@@ -17,7 +17,10 @@
 HALF = NZ // 2
 PLANE = 16
 PIECE = DIM // PLANE
-LAGS = (0, 1, 1, 2, 3, 3, 3, 3)
+LAGS = (0, 1, 1, 2, 2, 2, 2, 2)
+SIDE = 4
+STEPS = sorted(((dx, dy) for dy in range(SIDE) for dx in range(SIDE) if dx or dy),
+               key=lambda step: -sum(min(d, SIDE - d) for d in step))
 MESH = pl.DeviceIdType.MESH
 
 
@@ -35,6 +38,8 @@
     wide, core = lax.axis_index("wide"), lax.axis_index("narrow")
     here = wide % PLANE
     z = wide // PLANE
+    x, y = here % SIDE, here // SIDE
+    others = [(y + dy) % SIDE * SIDE + (x + dx) % SIDE for dx, dy in STEPS]
     partner = (wide, 1 - core)
     z_first = jnp.where(z < HALF, 0, 1)
     z_last = jnp.where(z < 2, HALF, NZ)
@@ -66,14 +71,14 @@
 
     with scope("a_sig"):
         barrier = pltpu.get_barrier_semaphore()
-        late = (z < HALF) | ((z < NZ - 1) & (here % 4 >= 2) & (here >= PLANE // 2))
+        late = jnp.where(z == 0, x + y > 1, jnp.where(z == 3, x + y > 2, (z < HALF) | ((z == HALF) & (x >= 2) & (y >= 2))))
 
         @pl.when(jnp.where(late, 1, 0) == core)
         def _():
             pl.semaphore_signal(barrier, inc=1, device_id=partner, device_id_type=MESH)
 
-        for i in range(1, PLANE):
-            pl.semaphore_signal(barrier, inc=1, device_id=(chip_in_plane((here + i) % PLANE), 0), device_id_type=MESH)
+        for chip in others:
+            pl.semaphore_signal(barrier, inc=1, device_id=(chip_in_plane(chip), 0), device_id_type=MESH)
 
         @pl.loop(z_first, z)
         def _(frm):
@@ -146,8 +151,7 @@
         with scope(f"f_up{k}"):
             total[rows(k)] = own[core, rows(k)] + part[rows(k)]
             up[slice_of(k, here)] = total[slice_of(k, here)]
-            for i in range(1, PLANE):
-                root = (here + i) % PLANE
+            for root in others:
                 remote(total.at[slice_of(k, root)], up.at[slice_of(k, here)], up_send, up_recv.at[k],
                        (chip_in_plane(root), core)).start()
 
@@ -207,8 +211,7 @@
             for i in range(PLANE):
                 down[slice_of(k, i)] = prefix[slice_of(k, i)] + above
             carry[slice_of(k, here)] = down[slice_of(k, here)]
-            for i in range(1, PLANE):
-                chip = (here + i) % PLANE
+            for chip in others:
                 remote(down.at[slice_of(k, chip)], carry.at[slice_of(k, here)], dn_send, dn_recv.at[k],
                        (chip_in_plane(chip), core)).start()
 

time: 27.8 us -> 27.3 us (0.982)
  Pallas kernels: 26.9 us -> 26.4 us
    pallas_call x1, Pallas kernels: 26.9 us -> 26.4 us  [shards(): pl.pallas_call(kernel, out_shape=pltpu.VMEM(queries.shape, queries.dtype)...]
where the time goes in v4:
time: 27.3 us; the launch traced here: 27.2 us
  Pallas kernels  26.4 us (97%)
  local copies, waits for them, and re-layouts  0.8 us (3%)
    pallas_call x1, Pallas kernels, shards(): pl.pallas_call(kernel, out_shape=pltpu.VMEM(queries.shape, queries.dtype)...  26.4 us
    unnamed x1, local copies, waits for them, and re-layouts  0.8 us

profile of v4, /device:TPU:225, one launch (start us, length us, event | category | flops | bytes accessed | tf_op | source)
XLA Modules:
  0.0 27.2 jit_solution(2057774416587295902)
XLA Ops:
  0.0 26.4 %prefix_attention.1 = bf16[128,2048]{1,0:T(8,128)(2,1)S(1)} custom-call(bf16[128,2048]{1,0:T(8,128)(2,1)} %q_hbm.1, bf16[128,2048]{1,0:T(8,128)(2,1)} %k_hbm.1, bf16[128,2048]{1,0:T(8,128)(2,1)} %v_hbm.1), custom_call_target="tpu_custom_call" | custom-call | tf_op jit(solution)/shard_map/prefix_attention/pallas_call | solution.py:275
  26.4 0.8 %copy.5 = bf16[128,2048]{1,0:T(8,128)(2,1)} copy(bf16[128,2048]{1,0:T(8,128)(2,1)S(1)} %prefix_attention.1) | data formatting | bytes 1048576

commit v5 on v4

--- a/solution.py
+++ b/solution.py
@@ -80,16 +80,18 @@
         for chip in others:
             pl.semaphore_signal(barrier, inc=1, device_id=(chip_in_plane(chip), 0), device_id_type=MESH)
 
-        @pl.loop(z_first, z)
-        def _(frm):
-            pl.semaphore_signal(barrier, inc=1, device_id=(frm * PLANE + here, 1), device_id_type=MESH)
+        @pl.when(core == 1)
+        def _():
+            @pl.loop(z_first, z)
+            def _(frm):
+                pl.semaphore_signal(barrier, inc=1, device_id=(frm * PLANE + here, 1), device_id_type=MESH)
 
         loads = [pltpu.make_async_copy(src, dst, in_sem.at[i])
                  for i, (src, dst) in enumerate(((k_hbm, k_ref), (v_hbm, v_ref), (q_hbm, q_ref)))]
         for load in loads:
             load.start()
 
-    z_peers = 2 * (z_last - 1 - z + jnp.where(z == 1, NZ - HALF, 0))
+    z_peers = z_last - 1 - z + jnp.where(z == 1, NZ - HALF, 0)
 
     def meet_above(count):
         @pl.when(core == 1)
@@ -150,10 +152,17 @@
                 arrived(part.at[pl.ds(CHUNKS[k][0] * DIM, rest * DIM)], ex_recv.at[k])
         with scope(f"f_up{k}"):
             total[rows(k)] = own[core, rows(k)] + part[rows(k)]
-            up[slice_of(k, here)] = total[slice_of(k, here)]
             for root in others:
-                remote(total.at[slice_of(k, root)], up.at[slice_of(k, here)], up_send, up_recv.at[k],
-                       (chip_in_plane(root), core)).start()
+                remote(total.at[slice_of(k, root)], up.at[core, slice_of(k, here)], up_send, up_recv.at[core, k],
+                       (chip_in_plane(root), 1)).start()
+
+            @pl.when(core == 0)
+            def _():
+                remote(total.at[slice_of(k, here)], up.at[0, slice_of(k, here)], up_send, up_recv.at[0, k], partner).start()
+
+            @pl.when(core == 1)
+            def _():
+                up[1, slice_of(k, here)] = total[slice_of(k, here)]
 
     with scope("g_local"):
         loads[2].wait()
@@ -165,67 +174,72 @@
             local[:, at] = dot(scores, v_ref[:, at], ((1,), (0,)))
 
     with scope("g_meet"):
-        @pl.when(late)
-        def _():
-            meet_above(z_peers)
-
-    def to_plane(source, k, to):
-        return remote(source.at[root_rows(k)], zrecv.at[z, root_rows(k)], z_send, z_recv.at[k],
-                      (to * PLANE + here, core))
-
-    def root(k):
-        with scope(f"h_upwait{k}"):
-            arrived(up.at[all_but_one(k)], up_recv.at[k])
-        with scope(f"h_root{k}"):
+        @pl.when(late & (core == 1))
+        def _():
+            pl.semaphore_wait(barrier, z_peers)
+
+    def to_plane(source, g, k, to):
+        return remote(source.at[g, root_rows(k)], zrecv.at[g, z, root_rows(k)], z_send, z_recv.at[g, k],
+                      (to * PLANE + here, 1))
+
+    def root(g, k):
+        with scope(f"h_upwait{k}_{g}"):
+            arrived(up.at[g, all_but_one(k) if g else rows(k)], up_recv.at[g, k])
+        with scope(f"h_root{k}_{g}"):
             before = jnp.zeros((CHUNKS[k][1] * PIECE, DIM), jnp.float32)
             for i in range(PLANE):
-                prefix[slice_of(k, i)] = before
-                before = before + up[slice_of(k, i)]
-            plane[root_rows(k)] = before
+                prefix[g, slice_of(k, i)] = before
+                before = before + up[g, slice_of(k, i)]
+            plane[g, root_rows(k)] = before
 
             @pl.loop(z + 1, z_last)
             def _(to):
-                to_plane(plane, k, to).start()
-
-    def planes_arrived(count, at, sem):
-        for n in range(1, NZ - 1):
-            @pl.when(count == n)
-            def _():
-                arrived(zrecv.at[pl.ds(0, n), at], sem)
-
-    def earlier(k):
-        with scope(f"i_zwait{k}"):
-            planes_arrived(z - z_first, root_rows(k), z_recv.at[k])
-            below[root_rows(k)] = lax.fori_loop(z_first, z, lambda frm, acc: acc + zrecv[frm, root_rows(k)],
-                                                jnp.zeros((CHUNKS[k][1] * PIECE, DIM), jnp.float32))
+                to_plane(plane, g, k, to).start()
+
+    def earlier(g, k):
+        with scope(f"i_zwait{k}_{g}"):
+            for n in range(1, NZ - 1):
+                @pl.when(z - z_first == n)
+                def _():
+                    arrived(zrecv.at[g, pl.ds(0, n), root_rows(k)], z_recv.at[g, k])
+
+            below[g, root_rows(k)] = lax.fori_loop(z_first, z, lambda frm, acc: acc + zrecv[g, frm, root_rows(k)],
+                                                   jnp.zeros((CHUNKS[k][1] * PIECE, DIM), jnp.float32))
 
         @pl.when(z == 1)
         def _():
-            pair[root_rows(k)] = below[root_rows(k)] + plane[root_rows(k)]
+            pair[g, root_rows(k)] = below[g, root_rows(k)] + plane[g, root_rows(k)]
             for to in range(HALF, NZ):
-                to_plane(pair, k, to).start()
-
-    def carries(k):
-        with scope(f"i_down{k}"):
-            above = below[root_rows(k)]
+                to_plane(pair, g, k, to).start()
+
+    def carries(g, k):
+        with scope(f"i_down{k}_{g}"):
+            above = below[g, root_rows(k)]
             for i in range(PLANE):
-                down[slice_of(k, i)] = prefix[slice_of(k, i)] + above
-            carry[slice_of(k, here)] = down[slice_of(k, here)]
+                down[g, slice_of(k, i)] = prefix[g, slice_of(k, i)] + above
             for chip in others:
-                remote(down.at[slice_of(k, chip)], carry.at[slice_of(k, here)], dn_send, dn_recv.at[k],
-                       (chip_in_plane(chip), core)).start()
-
-    for step in range(N + max(LAGS)):
-        if step < N:
-            root(step)
-        for lag in sorted(set(LAGS)):
-            if 0 <= step - lag < N:
-                wanted = [i for i in range(NZ) if LAGS[i] == lag]
-
-                @pl.when(functools.reduce(jnp.logical_or, [z == i for i in wanted]))
-                def _():
-                    earlier(step - lag)
-                    carries(step - lag)
+                remote(down.at[g, slice_of(k, chip)], carry.at[slice_of(k, here)], dn_send, dn_recv.at[k],
+                       (chip_in_plane(chip), g)).start()
+            if g:
+                carry[slice_of(k, here)] = down[g, slice_of(k, here)]
+            else:
+                remote(down.at[g, slice_of(k, here)], carry.at[slice_of(k, here)], dn_send, dn_recv.at[k], partner).start()
+
+    @pl.when(core == 1)
+    def _():
+        for step in range(N + max(LAGS)):
+            if step < N:
+                for g in (1, 0):
+                    root(g, step)
+            for lag in sorted(set(LAGS)):
+                if 0 <= step - lag < N:
+                    wanted = [i for i in range(NZ) if LAGS[i] == lag]
+
+                    @pl.when(functools.reduce(jnp.logical_or, [z == i for i in wanted]))
+                    def _():
+                        for g in (1, 0):
+                            earlier(g, step - lag)
+                            carries(g, step - lag)
 
     def finish(group, head, state):
         at = columns(group, head)
@@ -246,7 +260,13 @@
 
     for k in range(N):
         with scope(f"j_dnwait{k}"):
-            arrived(carry.at[all_but_one(k)], dn_recv.at[k])
+            @pl.when(core == 0)
+            def _():
+                arrived(carry.at[rows(k)], dn_recv.at[k])
+
+            @pl.when(core == 1)
+            def _():
+                arrived(carry.at[all_but_one(k)], dn_recv.at[k])
         with scope(f"j_fin{k}"):
             give[rows(k)] = carry[rows(k)] + jnp.where(core == 0, own[core, rows(k)], 0.0)
             remote(give.at[rows(k)], other.at[rows(k)], fx_send, fx_recv.at[k], partner).start()
@@ -260,10 +280,21 @@
 
     with scope("l_waits"):
         arrived(own.at[1 - core], ex_send)
-        arrived(total.at[pl.ds(0, (PLANE - 1) * GROUP * PIECE)], up_send)
-        arrived(down.at[pl.ds(0, (PLANE - 1) * GROUP * PIECE)], dn_send)
+        @pl.when(core == 0)
+        def _():
+            arrived(total, up_send)
+
         arrived(give, fx_send)
-        planes_arrived(z_last - 1 - z + jnp.where(z == 1, NZ - HALF, 0), pl.ds(0, GROUP * PIECE), z_send)
+
+        @pl.when(core == 1)
+        def _():
+            most = (PLANE - 1) * GROUP * PIECE
+            arrived(total.at[pl.ds(0, most)], up_send)
+            arrived(down.reshape(2 * GROUP * DIM, DIM).at[pl.ds(0, GROUP * DIM + most)], dn_send)
+            for n in range(1, NZ - 1):
+                @pl.when(z_peers == n)
+                def _():
+                    arrived(zrecv.at[:, pl.ds(0, n)], z_send)
 
 
 def shards(queries, keys, values):
@@ -271,7 +302,8 @@
     hbm = pl.BlockSpec(memory_space=pltpu.HBM)
     block = pltpu.VMEM(queries.shape, queries.dtype)
     state = pltpu.VMEM((GROUP * DIM, DIM), jnp.float32)
-    root = pltpu.VMEM((GROUP * PIECE, DIM), jnp.float32)
+    states = pltpu.VMEM((2, GROUP * DIM, DIM), jnp.float32)
+    root = pltpu.VMEM((2, GROUP * PIECE, DIM), jnp.float32)
     return pl.pallas_call(
         kernel,
         out_shape=pltpu.VMEM(queries.shape, queries.dtype),
@@ -279,13 +311,12 @@
         out_specs=pl.BlockSpec(memory_space=pltpu.VMEM),
         scratch_shapes=[
             block, block, block,
-            pltpu.VMEM((2, GROUP * DIM, DIM), jnp.float32),
-            state, state, state, state, root, root, root,
-            pltpu.VMEM((NZ, GROUP * PIECE, DIM), jnp.float32),
-            state, state, state, state,
+            states, state, state, states, states, root, root, root,
+            pltpu.VMEM((2, NZ, GROUP * PIECE, DIM), jnp.float32),
+            states, state, state, state,
             pltpu.VMEM((DIM, HEADS * DIM), jnp.float32),
             dma((3,)), pltpu.SemaphoreType.REGULAR, pltpu.SemaphoreType.REGULAR,
-            dma, dma((2,)), dma, dma((N,)), dma, dma((N,)), dma, dma((N,)), dma, dma((N,)),
+            dma, dma((2,)), dma, dma((2, N)), dma, dma((2, N)), dma, dma((N,)), dma, dma((N,)),
         ],
         compiler_params=pltpu.CompilerParams(collective_id=0, has_side_effects=True),
         name="prefix_attention",

time: 27.3 us -> 26.4 us (0.967); the launches traced: 27.2 us -> 25.9 us
  Pallas kernels: 26.4 us -> 25.1 us
    pallas_call x1, Pallas kernels: 26.4 us -> 25.1 us  [shards(): pl.pallas_call(kernel, out_shape=pltpu.VMEM(queries.shape, queries.dtype)...]
where the time goes in v5:
time: 26.4 us; the launch traced here: 25.9 us
  Pallas kernels  25.1 us (95%)
  local copies, waits for them, and re-layouts  0.8 us (3%)
    pallas_call x1, Pallas kernels, shards(): pl.pallas_call(kernel, out_shape=pltpu.VMEM(queries.shape, queries.dtype)...  25.1 us
    unnamed x1, local copies, waits for them, and re-layouts  0.8 us

profile of v5, /device:TPU:225, one launch (start us, length us, event | category | flops | bytes accessed | tf_op | source)
XLA Modules:
  0.0 25.9 jit_solution(8551844943187100470)
XLA Ops:
  0.0 25.1 %prefix_attention.1 = bf16[128,2048]{1,0:T(8,128)(2,1)S(1)} custom-call(bf16[128,2048]{1,0:T(8,128)(2,1)} %q_hbm.1, bf16[128,2048]{1,0:T(8,128)(2,1)} %k_hbm.1, bf16[128,2048]{1,0:T(8,128)(2,1)} %v_hbm.1), custom_call_target="tpu_custom_call" | custom-call | tf_op jit(solution)/shard_map/prefix_attention/pallas_call | solution.py:307
  25.1 0.8 %copy.5 = bf16[128,2048]{1,0:T(8,128)(2,1)} copy(bf16[128,2048]{1,0:T(8,128)(2,1)S(1)} %prefix_attention.1) | data formatting | bytes 1048576

commit v6 on v5

--- a/solution.py
+++ b/solution.py
@@ -17,7 +17,7 @@
 HALF = NZ // 2
 PLANE = 16
 PIECE = DIM // PLANE
-LAGS = (0, 1, 1, 2, 2, 2, 2, 2)
+LAGS = (0, 1, 1, 1, 2, 2, 2, 2)
 SIDE = 4
 STEPS = sorted(((dx, dy) for dy in range(SIDE) for dx in range(SIDE) if dx or dy),
                key=lambda step: -sum(min(d, SIDE - d) for d in step))

time: 26.4 us -> 26.2 us (level)
  no operation moved by 1% of the time
where the time goes in v6:
time: 26.2 us; the launch traced here: 25.9 us
  Pallas kernels  25.1 us (96%)
  local copies, waits for them, and re-layouts  0.8 us (3%)
    pallas_call x1, Pallas kernels, shards(): pl.pallas_call(kernel, out_shape=pltpu.VMEM(queries.shape, queries.dtype)...  25.1 us
    unnamed x1, local copies, waits for them, and re-layouts  0.8 us

profile of v6, /device:TPU:225, one launch (start us, length us, event | category | flops | bytes accessed | tf_op | source)
XLA Modules:
  0.0 25.9 jit_solution(13699819832426296890)
XLA Ops:
  0.0 25.1 %prefix_attention.1 = bf16[128,2048]{1,0:T(8,128)(2,1)S(1)} custom-call(bf16[128,2048]{1,0:T(8,128)(2,1)} %q_hbm.1, bf16[128,2048]{1,0:T(8,128)(2,1)} %k_hbm.1, bf16[128,2048]{1,0:T(8,128)(2,1)} %v_hbm.1), custom_call_target="tpu_custom_call" | custom-call | tf_op jit(solution)/shard_map/prefix_attention/pallas_call | solution.py:307
  25.1 0.8 %copy.5 = bf16[128,2048]{1,0:T(8,128)(2,1)} copy(bf16[128,2048]{1,0:T(8,128)(2,1)S(1)} %prefix_attention.1) | data formatting | bytes 1048576

commit v7 on v6

--- a/solution.py
+++ b/solution.py
@@ -11,7 +11,7 @@
 HEADS = 16
 DIM = 128
 GROUP = HEADS // 2
-CHUNKS = ((0, 2), (2, 2), (4, 2), (6, 1), (7, 1))
+CHUNKS = ((0, 1), (1, 2), (3, 2), (5, 2), (7, 1))
 N = len(CHUNKS)
 NZ = 8
 HALF = NZ // 2
@@ -228,16 +228,15 @@
     @pl.when(core == 1)
     def _():
         for step in range(N + max(LAGS)):
-            if step < N:
-                for g in (1, 0):
+            for g in (1, 0):
+                if step < N:
                     root(g, step)
-            for lag in sorted(set(LAGS)):
-                if 0 <= step - lag < N:
-                    wanted = [i for i in range(NZ) if LAGS[i] == lag]
-
-                    @pl.when(functools.reduce(jnp.logical_or, [z == i for i in wanted]))
-                    def _():
-                        for g in (1, 0):
+                for lag in sorted(set(LAGS)):
+                    if 0 <= step - lag < N:
+                        wanted = [i for i in range(NZ) if LAGS[i] == lag]
+
+                        @pl.when(functools.reduce(jnp.logical_or, [z == i for i in wanted]))
+                        def _():
                             earlier(g, step - lag)
                             carries(g, step - lag)
 

time: 26.2 us -> 26 us (level)
  no operation moved by 1% of the time
where the time goes in v7:
time: 26 us; the launch traced here: 25.9 us
  Pallas kernels  25.1 us (97%)
  local copies, waits for them, and re-layouts  0.8 us (3%)
    pallas_call x1, Pallas kernels, shards(): pl.pallas_call(kernel, out_shape=pltpu.VMEM(queries.shape, queries.dtype)...  25.1 us
    unnamed x1, local copies, waits for them, and re-layouts  0.8 us

profile of v7, /device:TPU:225, one launch (start us, length us, event | category | flops | bytes accessed | tf_op | source)
XLA Modules:
  0.0 25.9 jit_solution(10275332737676004918)
XLA Ops:
  0.0 25.1 %prefix_attention.1 = bf16[128,2048]{1,0:T(8,128)(2,1)S(1)} custom-call(bf16[128,2048]{1,0:T(8,128)(2,1)} %q_hbm.1, bf16[128,2048]{1,0:T(8,128)(2,1)} %k_hbm.1, bf16[128,2048]{1,0:T(8,128)(2,1)} %v_hbm.1), custom_call_target="tpu_custom_call" | custom-call | tf_op jit(solution)/shard_map/prefix_attention/pallas_call | solution.py:306
  25.1 0.8 %copy.5 = bf16[128,2048]{1,0:T(8,128)(2,1)} copy(bf16[128,2048]{1,0:T(8,128)(2,1)S(1)} %prefix_attention.1) | data formatting | bytes 1048576

commit v8 on v7

--- a/solution.py
+++ b/solution.py
@@ -192,9 +192,9 @@
                 before = before + up[g, slice_of(k, i)]
             plane[g, root_rows(k)] = before
 
-            @pl.loop(z + 1, z_last)
-            def _(to):
-                to_plane(plane, g, k, to).start()
+            @pl.loop(0, z_last - 1 - z)
+            def _(n):
+                to_plane(plane, g, k, z_last - 1 - n).start()
 
     def earlier(g, k):
         with scope(f"i_zwait{k}_{g}"):
@@ -217,9 +217,13 @@
             above = below[g, root_rows(k)]
             for i in range(PLANE):
                 down[g, slice_of(k, i)] = prefix[g, slice_of(k, i)] + above
-            for chip in others:
-                remote(down.at[g, slice_of(k, chip)], carry.at[slice_of(k, here)], dn_send, dn_recv.at[k],
-                       (chip_in_plane(chip), g)).start()
+            for late_ones in (False, True):
+                for chip in others:
+                    @pl.when(((chip % SIDE >= 2) & (chip >= PLANE // 2)) == late_ones)
+                    def _():
+                        remote(down.at[g, slice_of(k, chip)], carry.at[slice_of(k, here)], dn_send, dn_recv.at[k],
+                               (chip_in_plane(chip), g)).start()
+
             if g:
                 carry[slice_of(k, here)] = down[g, slice_of(k, here)]
             else:

time: 26 us -> 25.7 us (0.988)
  Pallas kernels: 25.1 us -> 24.8 us
where the time goes in v8:
time: 25.7 us; the launch traced here: 25.6 us
  Pallas kernels  24.8 us (96%)
  local copies, waits for them, and re-layouts  0.8 us (3%)
    pallas_call x1, Pallas kernels, shards(): pl.pallas_call(kernel, out_shape=pltpu.VMEM(queries.shape, queries.dtype)...  24.8 us
    unnamed x1, local copies, waits for them, and re-layouts  0.8 us

profile of v8, /device:TPU:225, one launch (start us, length us, event | category | flops | bytes accessed | tf_op | source)
XLA Modules:
  0.0 25.6 jit_solution(4312497366993262370)
XLA Ops:
  0.0 24.8 %prefix_attention.1 = bf16[128,2048]{1,0:T(8,128)(2,1)S(1)} custom-call(bf16[128,2048]{1,0:T(8,128)(2,1)} %q_hbm.1, bf16[128,2048]{1,0:T(8,128)(2,1)} %k_hbm.1, bf16[128,2048]{1,0:T(8,128)(2,1)} %v_hbm.1), custom_call_target="tpu_custom_call" | custom-call | tf_op jit(solution)/shard_map/prefix_attention/pallas_call | solution.py:310
  24.8 0.8 %copy.5 = bf16[128,2048]{1,0:T(8,128)(2,1)} copy(bf16[128,2048]{1,0:T(8,128)(2,1)S(1)} %prefix_attention.1) | data formatting | bytes 1048576
